TPU v7x, 32 devices: a whole 2x2x4 slice. The times are simulated.
32 devices in a mesh: batch: 8 (over z, y), seq: 4 (over x, core).
Axes of the slice: x: 2, y: 2, z: 4, core: 2. Of those that a mesh axis runs over, the one named last changes fastest.
Arguments:
- inputs: bfloat16 [16, 1024, 768], P('batch', 'seq'), may hold values from -6 to 6
- segments: int32 [16, 1024], P('batch'), may hold values from 0 to 7, never falling along the last dimension, each value on 1 to 512 neighbouring positions
- qkv_weight: bfloat16 [768, 2304], replicated, may hold values from -0.21875 to 0.21875
- query_bias: bfloat16 [768], replicated, may hold values from -3 to 3
- value_bias: bfloat16 [768], replicated, may hold values from -3 to 3
- out_weight: bfloat16 [768, 768], replicated, may hold values from -1.75 to 1.75
- out_bias: bfloat16 [768], replicated, may hold values from -3 to 3
- norm1_gain: bfloat16 [768], replicated, may hold values from 0.099609375 to 1.8984375
- norm1_shift: bfloat16 [768], replicated, may hold values from -3 to 3
- up_weight: bfloat16 [768, 3072], replicated, may hold values from -0.21875 to 0.21875
- up_bias: bfloat16 [3072], replicated, may hold values from -3 to 3
- down_weight: bfloat16 [3072, 768], replicated, may hold values from -0.109375 to 0.109375
- down_bias: bfloat16 [768], replicated, may hold values from -3 to 3
- norm2_gain: bfloat16 [768], replicated, may hold values from 0.099609375 to 1.8984375
- norm2_shift: bfloat16 [768], replicated, may hold values from -3 to 3
- cotangent: bfloat16 [16, 1024, 768], P('batch', 'seq'), may hold values from -6 to 6
Outputs:
- outputs: bfloat16 [16, 1024, 768], P('batch', 'seq')
- input_grad: float32 [16, 1024, 768], P('batch', 'seq')
- qkv_weight_grad: float32 [768, 2304], P('batch', 'seq')
- query_bias_grad: float32 [768], replicated
- value_bias_grad: float32 [768], replicated
- out_weight_grad: float32 [768, 768], P('batch', 'seq')
- out_bias_grad: float32 [768], replicated
- norm1_gain_grad: float32 [768], replicated
- norm1_shift_grad: float32 [768], replicated
- up_weight_grad: float32 [768, 3072], P('batch', 'seq')
- up_bias_grad: float32 [3072], replicated
- down_weight_grad: float32 [3072, 768], P('batch', 'seq')
- down_bias_grad: float32 [768], replicated
- norm2_gain_grad: float32 [768], replicated
- norm2_shift_grad: float32 [768], replicated
Inputs may be any that keep to these rules, and one draw needn't show every extreme that they name: `segments`: in each packed row the passage numbers never fall, every number below 8 occurs, each passage holds 1 to 512 positions, and one passage in each row holds exactly 512.
All inputs are finite; a program needn't handle non-finite values.
Results may differ from a plain program's by a relative error of at most 0.013.
The roundings to bfloat16 on the way count: a program that leaves them out, or rounds other values in their place, can miss the bound.
Values may be sent and summed in bfloat16 or wider, within the bound.
No kernel may reach another device: no remote copies, remote signals or barrier semaphores. Data moves between devices by JAX's collectives and lax.ppermute only.
A program may use at most 192 MiB of HBM per device.

v0:
```python
import jax
import jax.numpy as jnp
from jax import lax
from jax.sharding import PartitionSpec as P

DH = 64
EPS = 1e-05
NEG = -1000000000.0


def layer_norm(values, gain, shift):
    mean = jnp.mean(values, axis=-1, keepdims=True)
    centred = values - mean
    spread = jnp.mean(centred * centred, axis=-1, keepdims=True)
    return centred * lax.rsqrt(spread + EPS) * gain + shift


def gelu_exact(values):
    return jax.nn.gelu(values, approximate=False)


def row_scores(query, keys, segment):
    scores = jnp.einsum("qhd,khd->hqk", query, keys, preferred_element_type=jnp.float32) * DH ** (
        -0.5
    )
    same = segment[:, None] == segment[None, :]
    return jnp.where(same[None], scores, NEG)


def attend_row(parts):
    query, keys, values, segment = parts
    scores = row_scores(query, keys, segment)
    top = jnp.max(scores, axis=-1, keepdims=True)
    expo = jnp.exp(scores - top)
    total = jnp.sum(expo, axis=-1, keepdims=True)
    probs = (expo / total).astype(jnp.bfloat16)
    context = jnp.einsum("hqk,khd->qhd", probs, values, preferred_element_type=jnp.float32)
    return (context.astype(jnp.bfloat16), (top + jnp.log(total))[..., 0])


def attend_back(parts):
    query, keys, values, segment, logsum, d_context = parts
    scores = row_scores(query, keys, segment)
    probs = jnp.exp(scores - logsum[..., None])
    d_values = jnp.einsum(
        "hqk,qhd->khd", probs.astype(jnp.bfloat16), d_context, preferred_element_type=jnp.float32
    )
    d_probs = jnp.einsum("qhd,khd->hqk", d_context, values, preferred_element_type=jnp.float32)
    delta = jnp.sum(probs * d_probs, axis=-1, keepdims=True)
    d_scores = (probs * (d_probs - delta)).astype(jnp.bfloat16)
    d_query = jnp.einsum(
        "hqk,khd->qhd", d_scores, keys, preferred_element_type=jnp.float32
    ) * DH ** (-0.5)
    d_keys = jnp.einsum(
        "hqk,qhd->khd", d_scores, query, preferred_element_type=jnp.float32
    ) * DH ** (-0.5)
    return jnp.stack([d_query, d_keys, d_values], axis=1).astype(jnp.bfloat16)


def body(
    inputs,
    segments,
    qkv_weight,
    query_bias,
    value_bias,
    out_weight,
    out_bias,
    norm1_gain,
    norm1_shift,
    up_weight,
    up_bias,
    down_weight,
    down_bias,
    norm2_gain,
    norm2_shift,
    cotangent,
):
    rows, local_len, width = inputs.shape
    count = rows * local_len
    flat_in = inputs.reshape(count, width)
    qkv_shift = jnp.concatenate(
        [
            query_bias.astype(jnp.float32),
            jnp.zeros((width,), jnp.float32),
            value_bias.astype(jnp.float32),
        ]
    )
    projected = (
        jnp.dot(flat_in, qkv_weight, preferred_element_type=jnp.float32) + qkv_shift
    ).astype(jnp.bfloat16)
    heads_in = lax.all_to_all(
        projected.reshape(rows, local_len, 3, width), "seq", split_axis=3, concat_axis=1, tiled=True
    )
    full_len = heads_in.shape[1]
    per_head = heads_in.shape[3] // DH
    split = heads_in.reshape(rows, full_len, 3, per_head, DH)
    query = split[:, :, 0]
    keys = split[:, :, 1]
    values = split[:, :, 2]
    context, logsum = lax.map(attend_row, (query, keys, values, segments))
    context = context.reshape(rows, full_len, per_head * DH)
    regrouped = lax.all_to_all(context, "seq", split_axis=1, concat_axis=2, tiled=True)
    flat_ctx = regrouped.reshape(count, width)
    attn = jnp.dot(flat_ctx, out_weight, preferred_element_type=jnp.float32) + out_bias.astype(
        jnp.float32
    )
    summed = flat_in.astype(jnp.float32) + attn
    hidden, norm1_back = jax.vjp(
        layer_norm, summed, norm1_gain.astype(jnp.float32), norm1_shift.astype(jnp.float32)
    )
    hidden_low = hidden.astype(jnp.bfloat16)
    pre_act = jnp.dot(hidden_low, up_weight, preferred_element_type=jnp.float32) + up_bias.astype(
        jnp.float32
    )
    act, gelu_back = jax.vjp(gelu_exact, pre_act)
    act_low = act.astype(jnp.bfloat16)
    branch = jnp.dot(act_low, down_weight, preferred_element_type=jnp.float32) + down_bias.astype(
        jnp.float32
    )
    final, norm2_back = jax.vjp(
        layer_norm, hidden + branch, norm2_gain.astype(jnp.float32), norm2_shift.astype(jnp.float32)
    )
    outputs = final.astype(jnp.bfloat16).reshape(rows, local_len, width)
    d_final = cotangent.reshape(count, width).astype(jnp.float32)
    d_res_two, d_gain_two, d_shift_two = norm2_back(d_final)
    d_down_bias = jnp.sum(d_res_two, axis=0)
    d_branch = d_res_two.astype(jnp.bfloat16)
    d_down = jnp.einsum("ti,to->io", act_low, d_branch, preferred_element_type=jnp.float32)
    d_act = jnp.einsum("to,io->ti", d_branch, down_weight, preferred_element_type=jnp.float32)
    (d_pre,) = gelu_back(d_act)
    d_pre_low = d_pre.astype(jnp.bfloat16)
    d_up_bias = jnp.sum(d_pre_low.astype(jnp.float32), axis=0)
    d_up = jnp.einsum("ti,to->io", hidden_low, d_pre_low, preferred_element_type=jnp.float32)
    d_hidden = d_res_two + jnp.einsum(
        "to,io->ti", d_pre_low, up_weight, preferred_element_type=jnp.float32
    )
    d_summed, d_gain_one, d_shift_one = norm1_back(d_hidden)
    d_out_bias = jnp.sum(d_summed, axis=0)
    d_attn = d_summed.astype(jnp.bfloat16)
    d_out = jnp.einsum("ti,to->io", flat_ctx, d_attn, preferred_element_type=jnp.float32)
    d_context = jnp.einsum(
        "to,io->ti", d_attn, out_weight, preferred_element_type=jnp.float32
    ).astype(jnp.bfloat16)
    d_heads = lax.all_to_all(
        d_context.reshape(rows, local_len, width), "seq", split_axis=2, concat_axis=1, tiled=True
    )
    d_heads = d_heads.reshape(rows, full_len, per_head, DH)
    d_split = lax.map(attend_back, (query, keys, values, segments, logsum, d_heads))
    d_back = lax.all_to_all(
        d_split.reshape(rows, full_len, 3, per_head * DH),
        "seq",
        split_axis=1,
        concat_axis=3,
        tiled=True,
    )
    d_proj = d_back.reshape(count, 3 * width)
    d_query_bias = jnp.sum(d_proj[:, :width].astype(jnp.float32), axis=0)
    d_value_bias = jnp.sum(d_proj[:, 2 * width :].astype(jnp.float32), axis=0)
    d_qkv = jnp.einsum("ti,to->io", flat_in, d_proj, preferred_element_type=jnp.float32)
    d_inputs = d_summed + jnp.einsum(
        "to,io->ti", d_proj, qkv_weight, preferred_element_type=jnp.float32
    )
    mats_part = (
        lax.psum_scatter(d_qkv, "seq", scatter_dimension=1, tiled=True),
        lax.psum_scatter(d_out, "seq", scatter_dimension=1, tiled=True),
        lax.psum_scatter(d_up, "seq", scatter_dimension=1, tiled=True),
        lax.psum_scatter(d_down, "seq", scatter_dimension=1, tiled=True),
    )
    mats_done = (
        lax.psum_scatter(mats_part[0], "batch", scatter_dimension=0, tiled=True),
        lax.psum_scatter(mats_part[1], "batch", scatter_dimension=0, tiled=True),
        lax.psum_scatter(mats_part[2], "batch", scatter_dimension=0, tiled=True),
        lax.psum_scatter(mats_part[3], "batch", scatter_dimension=0, tiled=True),
    )
    qkv_total, out_total, up_total, down_total = mats_done
    vectors = lax.psum(
        (
            d_query_bias,
            d_value_bias,
            d_out_bias,
            d_gain_one,
            d_shift_one,
            d_up_bias,
            d_down_bias,
            d_gain_two,
            d_shift_two,
        ),
        ("batch", "seq"),
    )
    return (
        outputs,
        d_inputs.reshape(rows, local_len, width),
        qkv_total,
        vectors[0],
        vectors[1],
        out_total,
        vectors[2],
        vectors[3],
        vectors[4],
        up_total,
        vectors[5],
        down_total,
        vectors[6],
        vectors[7],
        vectors[8],
    )


def solution(mesh):
    placed = (
        P("batch", "seq", None),
        P("batch", None),
        P(),
        P(),
        P(),
        P(),
        P(),
        P(),
        P(),
        P(),
        P(),
        P(),
        P(),
        P(),
        P(),
        P("batch", "seq", None),
    )
    return jax.shard_map(
        body,
        mesh=mesh,
        in_specs=placed,
        out_specs=(
            P("batch", "seq", None),
            P("batch", "seq", None),
            P("batch", "seq"),
            P(),
            P(),
            P("batch", "seq"),
            P(),
            P(),
            P(),
            P("batch", "seq"),
            P(),
            P("batch", "seq"),
            P(),
            P(),
            P(),
        ),
        check_vma=False,
    )
```

profile of v0, /device:TPU:0, one launch (start us, length us, event | category | flops | bytes accessed | tf_op | source)
XLA Modules:
  0.0 870.2 jit_solution(6326495366198733760)
XLA Ops:
  9.2 4.6 fusion.60
  13.8 6.2 reshape.286
  20.0 8.8 %copy.104 = bf16[2,256,3,768]{1,0,2,3:T(2,128)(2,1)} copy(bf16[2,256,3,768]{3,2,1,0:T(4,128)(2,1)} %reshape.286) | data formatting | bytes 4718592 | tf_op jit(solution)/shard_map/reshape | solution.py:92
  28.8 4.5 all-to-all-start
  33.3 29.2 %all-to-all-done = bf16[2,256,3,768]{1,0,2,3:T(2,128)(2,1)} async-done(((bf16[2,256,3,768]{1,0,2,3:T(2,128)(2,1)}), bf16[2,256,3,768]{1,0,2,3:T(2,128)(2,1)}, u32[]{:S(2)}, u32[]{:S(2)}) %all-to-all-start) | async-done | bytes 2359328 | tf_op jit(solution)/shard_map/all_to_all | solution.py:91
  62.5 2.0 copy.105
  64.5 3.2 copy.106
  67.7 5.4 reshape.276
  73.2 3.1 slice_bitcast_fusion
  76.3 48.8 %while.22 = (s32[]{:T(128)}, bf16[2,1024,3,64]{1,3,2,0:T(8,128)(2,1)}, f32[2,3,1024]{2,1,0:T(4,128)}, bf16[2,1024,3,64]{1,3,2,0:T(8,128)(2,1)}, s32[2,1024]{1,0:...) while((s32[]{:T(128)}, ...), condition=%wide.region_3.4_spmd, body=%wide.region_0.3_spmd.sunk | while | flops 844297216 | bytes 46787188 | solution.py:100
  76.9 8.2 fusion.117
  85.2 7.4 fusion.118
  93.2 7.5 fusion.119
  101.4 8.2 fusion.117
  109.6 7.4 fusion.118
  117.6 7.5 fusion.119
  125.1 3.6 copy.107
  128.7 4.4 all-to-all-start.1
  140.3 7.4 all-to-all-done.1
  147.7 3.8 copy.124
  151.5 1.9 copy.109
  154.5 2.6 fusion.78
  157.5 19.6 %multiply_convert_fusion.1 = (bf16[512,3072]{1,0:T(8,128)(2,1)S(1)}, f32[512,3072]{1,0:T(8,128)}, f32[512,3072]{1,0:T(8,128)}) fusion(f32[3072]{0:T(1024)S(1)} %copy-done.26, bf16[768,3072]{1,0:T(8,128)(2,1)} %param.29, f32[512,768]{1,0:T(8,128)S(1)} %get-tuple-element.249, f32[768]{0:T(1024)S(1)} %copy-done.30, f32[768]{0:T(1024)S(1)} %copy-done.24, ...), kind=kOutput, calls=%fused_computation.68 | convolution fusion | flops 2521694208 | bytes 22042624 | tf_op jit(solution)/shard_map/dot_general | solution.py:112
  177.2 2.8 fusion.79
  181.7 1.6 fusion.76
  183.3 9.8 %convert_reduce_fusion = (f32[3072]{0:T(1024)}, bf16[512,3072]{1,0:T(8,128)(2,1)}) fusion(f32[512,3072]{1,0:T(8,128)} %get-tuple-element.239, bf16[3072,768]{1,0:T(8,128)(2,1)S(1)} %bitcast.193, f32[512,768]{1,0:T(8,128)S(1)} %get-tuple-element.237, f32[512]{0:T(512)S(1)} %negate_multiply_fusion.2, f32[512,3072]{1,0:T(8,128)} %get-tuple-element.250, ...), kind=kOutput, calls=%fused_computation.66 | convolution fusion | flops 2443441152 | bytes 22046720 | tf_op jit(solution)/shard_map/to,io->ti/dot_general | solution.py:129
  193.1 5.6 multiply_reduce_fusion.1
  200.6 1.8 convolution_convert_fusion
  202.4 3.0 copy.110
  205.4 4.2 all-to-all-start.2
  209.7 4.0 fusion.70
  213.8 7.6 all-to-all-done.2
  224.1 2.8 reshape.281
  226.9 57.5 %while.23 = (s32[]{:T(128)}, bf16[2,1024,3,3,64]{1,4,3,2,0:T(8,128)(2,1)}, bf16[2,1024,3,64]{1,3,2,0:T(8,128)(2,1)}, s32[2,1024]{1,0:T(2,128)S(1)}, bf16[2,1024,...) while((s32[]{:T(128)}, ...), condition=%wide.region_14.15_spmd, body=%wide.region_12.14_spmd.sunk | while | flops 2066019328 | bytes 119119104 | solution.py:148
  226.9 3.1 fusion.128
  231.4 7.2 multiply_reduce_fusion.6
  238.6 7.1 multiply_convert_fusion.3
  246.9 2.8 fusion.130
  249.7 4.8 fusion.129
  255.7 3.1 fusion.128
  260.2 7.2 multiply_reduce_fusion.6
  267.4 7.0 multiply_convert_fusion.3
  275.6 2.8 fusion.130
  278.4 4.8 fusion.129
  284.4 8.7 %copy.113 = bf16[2,1024,3,192]{3,0,2,1:T(2,128)(2,1)} copy(bf16[2,1024,3,192]{1,3,2,0:T(8,128)(2,1)} %bitcast.33) | data formatting | bytes 4718592 | tf_op jit(solution)/shard_map/reshape | solution.py:150
  293.1 42.5 %all_to_all.60 = bf16[2,1024,3,192]{3,0,2,1:T(2,128)(2,1)} all-to-all(bf16[2,1024,3,192]{3,0,2,1:T(2,128)(2,1)} %copy.113), channel_id=1, replica_groups=mesh['batch'=8,'seq'=4] {'seq'}, dimensions={1} | all-to-all | bytes 4718592 | tf_op jit(solution)/shard_map/all_to_all | solution.py:149
  335.6 9.1 %copy.125 = bf16[2,4,256,3,192]{2,1,4,3,0:T(4,128)(2,1)} copy(bf16[2,4,256,3,192]{4,0,3,2,1:T(2,128)(2,1)} %bitcast.176) | data formatting | bytes 4718592 | tf_op jit(solution)/shard_map/all_to_all | solution.py:149
  344.6 4.1 copy.115
  350.6 5.0 convolution_bitcast_fusion
  356.2 10.3 %fusion.68 = f32[3072,768]{0,1:T(8,128)} fusion(bf16[512,3072]{1,0:T(8,128)(2,1)} %copy-done.14, f32[512,768]{1,0:T(8,128)} %copy-done.7, f32[512]{0:T(512)S(1)} %copy-done.22), kind=kOutput, calls=%fused_computation.126 | convolution fusion | flops 2416705536 | bytes 14157824 | tf_op jit(solution)/shard_map/ti,to->io/dot_general | solution.py:128
  367.3 9.4 %fusion.71 = f32[768,3072]{1,0:T(8,128)} fusion(bf16[512,3072]{1,0:T(8,128)(2,1)} %get-tuple-element.255, f32[512,768]{1,0:T(8,128)} %copy-done.12, f32[768]{0:T(1024)} %convert_element_type.101, f32[768]{0:T(1024)S(1)} %copy-done.25, f32[512]{0:T(512)S(1)} %copy-done.28, f32[512]{0:T(512)S(1)} %copy-done.20), kind=kOutput, calls=%fused_computation.129 | convolution fusion | flops 2417885184 | bytes 14166016 | tf_op jit(solution)/shard_map/ti,to->io/dot_general | solution.py:133
  376.9 2.2 copy.128
  379.2 41.3 %reduce-scatter.13.cloned.1.call-done = f32[768,576]{0,1:T(8,128)} async-done(((f32[768,2304]{0,1:T(8,128)}), f32[768,576]{0,1:T(8,128)}) %reduce-scatter.13.cloned.1.call-update) | async-done | bytes 1769488 | tf_op jit(solution)/shard_map/reduce_scatter | solution.py:164
  420.4 2.9 copy.126
  423.4 78.1 %reduce-scatter.21.cloned.1.call-done = f32[3072,192]{0,1:T(8,128)} async-done(((f32[3072,768]{0,1:T(8,128)}), f32[3072,192]{0,1:T(8,128)}) %reduce-scatter.21.cloned.1.call-update) | async-done | bytes 2359312 | tf_op jit(solution)/shard_map/reduce_scatter | solution.py:167
  501.6 80.8 %reduce-scatter.17.cloned.1.call-done = f32[768,768]{1,0:T(8,128)} async-done(((f32[768,3072]{1,0:T(8,128)}), f32[768,768]{1,0:T(8,128)}) %reduce-scatter.17.cloned.1.call-update) | async-done | bytes 2359312 | tf_op jit(solution)/shard_map/reduce_scatter | solution.py:166
  583.9 2.2 add_reduce_fusion.1
  586.0 1.6 add_reduce_fusion
  588.5 41.3 %all-reduce = (f32[768]{0:T(1024)}, f32[768]{0:T(1024)}, f32[768]{0:T(1024)}, f32[768]{0:T(1024)}, f32[768]{0:T(1024)}, /*index=5*/f32[3072]{0:T(1024)}, f32[768]{0:T(1024)}, f32[768]{0:T(1024)}, f32[768]{0:T(1024)}) all-reduce(f32[768]{0:T(1024)} %get-tuple-element.193, ...), channel_id=1, replica_groups=mesh['batch'=8,'seq'=4] {'batch','seq'}, use_global_device_ids=true, to_apply=%region_18.19 | all-reduce | flops 9216 | bytes 73728 | tf_op jit(solution)/shard_map/psum | solution.py:176
  629.9 5.3 convolution_add_fusion.1
  635.2 13.6 %reduce-scatter.27.cloned.1.call-done = f32[96,192]{1,0:T(8,128)} async-done(((f32[768,192]{1,0:T(8,128)}), f32[96,192]{1,0:T(8,128)}) %reduce-scatter.27.cloned.1.call-update) | async-done | bytes 73744
  648.8 70.0 %reduce-scatter.25.cloned.1.call-done = f32[96,576]{1,0:T(8,128)} async-done(((f32[768,576]{1,0:T(8,128)}), f32[96,576]{1,0:T(8,128)}) %reduce-scatter.25.cloned.1.call-update) | async-done | bytes 221200
  718.8 72.0 %reduce-scatter.23.cloned.1.call-done = f32[384,192]{0,1:T(8,128)} async-done(((f32[3072,192]{0,1:T(8,128)}), f32[384,192]{0,1:T(8,128)}) %reduce-scatter.23.cloned.1.call-update) | async-done | bytes 294928 | tf_op jit(solution)/shard_map/reduce_scatter | solution.py:173
  790.7 72.1 %reduce-scatter.19.cloned.1.call-done = f32[96,768]{1,0:T(8,128)} async-done(((f32[768,768]{1,0:T(8,128)}), f32[96,768]{1,0:T(8,128)}) %reduce-scatter.19.cloned.1.call-update) | async-done | bytes 294928 | tf_op jit(solution)/shard_map/reduce_scatter | solution.py:172
  (153 shorter events, 32.9 us)
Async XLA Ops:
  7.2 2.0 copy-start
  28.8 33.7 %all-to-all-start = ((bf16[2,256,3,768]{1,0,2,3:T(2,128)(2,1)}), bf16[2,256,3,768]{1,0,2,3:T(2,128)(2,1)}, u32[]{:S(2)}, u32[]{:S(2)}) async-start(bf16[2,256,3,768]{1,0,2,3:T(2,128)(2,1)} %copy.104), calls=%async_computation | async-start | bytes 4718592 | tf_op jit(solution)/shard_map/all_to_all | solution.py:91
  73.2 3.1 copy-start.16
  85.2 8.0 copy-start.8
  109.6 8.0 copy-start.8
  125.1 11.9 %copy-start.29 = (bf16[3072]{0:T(1024)(128)(2,1)S(1)}, bf16[3072]{0:T(1024)(128)(2,1)}, u32[]{:S(2)}) copy-start(bf16[3072]{0:T(1024)(128)(2,1)} %param.30) | copy-start | bytes 18436
  128.7 19.0 %all-to-all-start.1 = ((bf16[2,1024,192]{2,0,1:T(2,128)(2,1)}), bf16[2,1024,192]{2,0,1:T(2,128)(2,1)}, u32[]{:S(2)}, u32[]{:S(2)}) async-start(bf16[2,1024,192]{2,0,1:T(2,128)(2,1)} %copy.107), calls=%async_computation.1 | async-start | bytes 2097152 | tf_op jit(solution)/shard_map/all_to_all | solution.py:102
  153.6 0.9 copy-start.13
  153.6 3.9 copy-start.24
  153.6 3.9 copy-start.26
  153.6 3.9 copy-start.30
  154.5 22.6 %slice-start = ((s8[4718592]{0:T(1024)(128)(4,1)}), s8[4194304]{0:T(1024)(128)(4,1)S(1)}, s32[]{:S(2)}) async-start(s8[4718592]{0:T(1024)(128)(4,1)} %bitcast.192), calls=%async_computation.20 | async-start | bytes 8388608
  157.1 41.7 %copy-start.12 = (f32[512,768]{1,0:T(8,128)}, f32[512,768]{1,0:T(8,128)S(1)}, u32[]{:S(2)}) copy-start(f32[512,768]{1,0:T(8,128)S(1)} %get-tuple-element.249) | copy-start | bytes 4718596
  157.1 41.6 %copy-start.19 = (f32[512]{0:T(512)}, f32[512]{0:T(512)S(1)}, u32[]{:S(2)}) copy-start(f32[512]{0:T(512)S(1)} %broadcast_multiply_fusion.1) | copy-start | bytes 6148
  157.5 41.3 %copy-start.27 = (f32[512]{0:T(512)}, f32[512]{0:T(512)S(1)}, u32[]{:S(2)}) copy-start(f32[512]{0:T(512)S(1)} %fusion.66) | copy-start | bytes 6148
  157.5 19.7 %copy-start.31 = (f32[768]{0:T(1024)S(1)}, f32[768]{0:T(1024)}, u32[]{:S(2)}) copy-start(f32[768]{0:T(1024)} %convert_element_type.105) | copy-start | bytes 9220
  157.5 19.7 %slice-start.1 = ((s8[4718592]{0:T(1024)(128)(4,1)}), s8[524288]{0:T(1024)(128)(4,1)S(1)}, s32[]{:S(2)}) async-start(s8[4718592]{0:T(1024)(128)(4,1)} %bitcast.192), calls=%async_computation.21 | async-start | bytes 1048576
  177.2 2.9 copy-start.14
  177.2 3.2 copy-start.11
  181.7 11.4 %slice-start.2 = ((s8[4718592]{0:T(1024)(128)(4,1)}), s8[4194304]{0:T(1024)(128)(4,1)S(1)}, s32[]{:S(2)}) async-start(s8[4718592]{0:T(1024)(128)(4,1)} %bitcast.194), calls=%async_computation.22 | async-start | bytes 8388608
  183.3 9.8 %copy-start.7 = (f32[512,768]{1,0:T(8,128)}, f32[512,768]{1,0:T(8,128)S(1)}, u32[]{:S(2)}) copy-start(f32[512,768]{1,0:T(8,128)S(1)} %get-tuple-element.237) | copy-start | bytes 4718596
  183.3 9.8 %copy-start.21 = (f32[512]{0:T(512)}, f32[512]{0:T(512)S(1)}, u32[]{:S(2)}) copy-start(f32[512]{0:T(512)S(1)} %negate_multiply_fusion.2) | copy-start | bytes 6148
  183.3 9.8 %slice-start.3 = ((s8[4718592]{0:T(1024)(128)(4,1)}), s8[524288]{0:T(1024)(128)(4,1)S(1)}, s32[]{:S(2)}) async-start(s8[4718592]{0:T(1024)(128)(4,1)} %bitcast.194), calls=%async_computation.23 | async-start | bytes 1048576
  198.8 1.8 copy-start.32
  199.5 1.1 copy-start.6
  199.5 10.2 %copy-start.17 = (f32[512]{0:T(512)}, f32[512]{0:T(512)S(1)}, u32[]{:S(2)}) copy-start(f32[512]{0:T(512)S(1)} %negate_multiply_fusion.1) | copy-start | bytes 6148
  205.4 15.9 %all-to-all-start.2 = ((bf16[2,256,768]{1,0,2:T(2,128)(2,1)}), bf16[2,256,768]{1,0,2:T(2,128)(2,1)}, u32[]{:S(2)}, u32[]{:S(2)}) async-start(bf16[2,256,768]{1,0,2:T(2,128)(2,1)} %copy.110), calls=%async_computation.2 | async-start | bytes 1572864 | tf_op jit(solution)/shard_map/all_to_all | solution.py:144
  209.6 167.3 %reduce-scatter.15.cloned.1.call-start = ((), (), s32[]{:S(2)}) async-start(), calls=%async_computation.13 | async-start | bytes 2949120 | tf_op jit(solution)/shard_map/reduce_scatter | solution.py:165
  213.7 206.7 %reduce-scatter.13.cloned.1.call-start = ((), (), s32[]{:S(2)}) async-start(), calls=%async_computation.12 | async-start | bytes 8847360 | tf_op jit(solution)/shard_map/reduce_scatter | solution.py:164
  226.9 4.5 copy-start.9
  226.9 4.5 copy-start.10
  238.5 7.1 copy-start.2
  245.7 1.2 copy-start.3
  249.7 4.8 copy-start.1
  255.7 4.5 copy-start.9
  255.7 4.5 copy-start.10
  267.4 7.0 copy-start.2
  274.4 1.2 copy-start.3
  278.4 4.8 copy-start.1
  348.7 1.9 copy-start.15
  349.2 1.4 copy-start.4
  355.6 0.7 copy-start.22
  355.6 145.9 %reduce-scatter.21.cloned.1.call-start = ((), (), s32[]{:S(2)}) async-start(), calls=%async_computation.16 | async-start | bytes 11796480 | tf_op jit(solution)/shard_map/reduce_scatter | solution.py:167
  366.6 0.7 copy-start.20
  366.6 0.7 copy-start.25
  366.6 0.8 copy-start.28
  366.6 215.8 %reduce-scatter.17.cloned.1.call-start = ((), (), s32[]{:S(2)}) async-start(), calls=%async_computation.14 | async-start | bytes 11796480 | tf_op jit(solution)/shard_map/reduce_scatter | solution.py:166
  376.8 272.0 %reduce-scatter.27.cloned.1.call-start = ((), (), s32[]{:S(2)}) async-start(), calls=%async_computation.19 | async-start | bytes 884736
  379.1 339.7 %reduce-scatter.25.cloned.1.call-start = ((), (), s32[]{:S(2)}) async-start(), calls=%async_computation.18 | async-start | bytes 2211840
  423.3 367.4 %reduce-scatter.23.cloned.1.call-start = ((), (), s32[]{:S(2)}) async-start(), calls=%async_computation.17 | async-start | bytes 2654208 | tf_op jit(solution)/shard_map/reduce_scatter | solution.py:173
  501.5 84.6 %copy-start.18 = (f32[512]{0:T(512)S(1)}, f32[512]{0:T(512)}, u32[]{:S(2)}) copy-start(f32[512]{0:T(512)} %copy-done.17) | copy-start | bytes 6148
  501.5 361.4 %reduce-scatter.19.cloned.1.call-start = ((), (), s32[]{:S(2)}) async-start(), calls=%async_computation.15 | async-start | bytes 2654208 | tf_op jit(solution)/shard_map/reduce_scatter | solution.py:172
  582.4 6.1 copy-start.23
  582.4 5.2 copy-start.5
Sparse Core Ops, SparseCore 0:
  213.8 35.5 reduce-scatter.14
  355.7 64.6 reduce-scatter.12
  423.0 78.4 reduce-scatter.20
  503.9 78.4 reduce-scatter.16
  586.1 62.6 reduce-scatter.26
  653.1 65.6 reduce-scatter.24
  722.8 67.8 reduce-scatter.22
  794.8 68.0 reduce-scatter.18
where the time goes:
time: 882 us; the launch traced here: 870 us
  waiting for transfers between devices  472 us (54%)
  matrix products  150 us (17%)
  blocking collectives  83.8 us (10%)
  local copies, waits for them, and re-layouts  81 us (9%)
  other arithmetic  54.1 us (6%)
  between operations  15 us (2%)
  starting transfers between devices  13.5 us (2%)
    unnamed x10, waiting for transfers between devices  83.7 us
    reduce_scatter x1, waiting for transfers between devices, body(): lax.psum_scatter(d_up, 'seq', scatter_dimension=1, tiled=True)  80.8 us
    reduce_scatter x1, waiting for transfers between devices, body(): lax.psum_scatter(d_down, 'seq', scatter_dimension=1, tiled=True)  78.1 us
    reduce_scatter x1, waiting for transfers between devices, body(): lax.psum_scatter(mats_part[2], 'batch', scatter_dimension=0, tiled=True)  72.1 us
    reduce_scatter x1, waiting for transfers between devices, body(): lax.psum_scatter(mats_part[3], 'batch', scatter_dimension=0, tiled=True)  72 us
    all_to_all x1, blocking collectives, body(): lax.all_to_all(d_split.reshape(rows, full_len, 3, per_head * DH), 'seq',...  42.5 us
    psum x1, blocking collectives, body(): lax.psum((d_query_bias, d_value_bias, d_out_bias, d_gain_one, d_shift_one...  41.3 us
    reduce_scatter x1, waiting for transfers between devices, body(): lax.psum_scatter(d_qkv, 'seq', scatter_dimension=1, tiled=True)  41.3 us
  transfers between devices with their start and end apart: 11, of which 10 were waited for; matrix products, arithmetic and copies ran while one was open for 16% of the time, Pallas kernels for 0%

commit v1 on v0

--- a/solution.py
+++ b/solution.py
@@ -6,6 +6,29 @@
 DH = 64
 EPS = 1e-05
 NEG = -1000000000.0
+
+
+def cut_along(x, dim, count):
+    dims = x.shape
+    blocks = x.reshape(*dims[:dim], count, dims[dim] // count, *dims[dim + 1 :])
+    return jnp.moveaxis(blocks, dim, 0)
+
+
+def joined_along(blocks, dim):
+    shape = list(blocks.shape[1:])
+    shape[dim] *= blocks.shape[0]
+    return jnp.moveaxis(blocks, 0, dim).reshape(shape)
+
+
+def pairwise_exchange(value, axis, split_dim, concat_dim):
+    size, place = (lax.axis_size(axis), lax.axis_index(axis))
+    pieces = cut_along(value, split_dim, size)
+    done = [pieces[place]]
+    for step in range(1, size):
+        sent = pieces[place ^ step]
+        done.append(lax.ppermute(sent, axis, [(i, i ^ step) for i in range(size)]))
+    pieces = jnp.stack(done)[place ^ jnp.arange(size)]
+    return joined_along(pieces, concat_dim)
 
 
 def layer_norm(values, gain, shift):
@@ -88,9 +111,7 @@
     projected = (
         jnp.dot(flat_in, qkv_weight, preferred_element_type=jnp.float32) + qkv_shift
     ).astype(jnp.bfloat16)
-    heads_in = lax.all_to_all(
-        projected.reshape(rows, local_len, 3, width), "seq", split_axis=3, concat_axis=1, tiled=True
-    )
+    heads_in = pairwise_exchange(projected.reshape(rows, local_len, 3, width), "seq", 3, 1)
     full_len = heads_in.shape[1]
     per_head = heads_in.shape[3] // DH
     split = heads_in.reshape(rows, full_len, 3, per_head, DH)

time: 882 us -> 882 us (level)
    all_to_all x1 -> x0, waiting for transfers between devices: 29.2 us -> none  [body(): lax.all_to_all(projected.reshape(rows, local_len, 3, width), 'seq', split...]
    ppermute x0 -> x3, waiting for transfers between devices: none -> 24.5 us  [pairwise_exchange(): done.append(lax.ppermute(sent, axis, [(i, i ^ step) for i in range(size)]))]
    reshape x3 -> x0, local copies, waits for them, and re-layouts: 20.5 us -> none  [the longest x2 15 us: body(): projected.reshape(rows, local_len, 3, width)]
    another operation x0 -> x7, local copies, waits for them, and re-layouts: none -> 19.4 us
  transfers between devices with their start and end apart: 11 -> 13, of which waited for: 10 -> 11; matrix products, arithmetic and copies ran while one was open for 16% -> 16% of each run, Pallas kernels for 0% -> 0%
where the time goes in v1:
time: 882 us; the launch traced here: 873 us
  waiting for transfers between devices  468 us (53%)
  matrix products  150 us (17%)
  local copies, waits for them, and re-layouts  87.5 us (10%)
  blocking collectives  83.7 us (9%)
  other arithmetic  57.3 us (6%)
  between operations  14.8 us (2%)
  starting transfers between devices  12 us (1%)
    unnamed x10, waiting for transfers between devices  83.7 us
    reduce_scatter x1, waiting for transfers between devices, body(): lax.psum_scatter(d_up, 'seq', scatter_dimension=1, tiled=True)  80.8 us
    reduce_scatter x1, waiting for transfers between devices, body(): lax.psum_scatter(d_down, 'seq', scatter_dimension=1, tiled=True)  78.1 us
    reduce_scatter x1, waiting for transfers between devices, body(): lax.psum_scatter(mats_part[2], 'batch', scatter_dimension=0, tiled=True)  72.3 us
    reduce_scatter x1, waiting for transfers between devices, body(): lax.psum_scatter(mats_part[3], 'batch', scatter_dimension=0, tiled=True)  72 us
    all_to_all x1, blocking collectives, body(): lax.all_to_all(d_split.reshape(rows, full_len, 3, per_head * DH), 'seq',...  42.5 us
    psum x1, blocking collectives, body(): lax.psum((d_query_bias, d_value_bias, d_out_bias, d_gain_one, d_shift_one...  41.3 us
    reduce_scatter x1, waiting for transfers between devices, body(): lax.psum_scatter(d_qkv, 'seq', scatter_dimension=1, tiled=True)  41.1 us
  transfers between devices with their start and end apart: 13, of which 11 were waited for; matrix products, arithmetic and copies ran while one was open for 16% of the time, Pallas kernels for 0%

profile of v1, /device:TPU:0, one launch (start us, length us, event | category | flops | bytes accessed | tf_op | source)
XLA Modules:
  0.0 873.1 jit_solution(4506528530854525369)
XLA Ops:
  9.2 4.5 fusion.60
  13.8 4.3 copy.112
  18.0 6.0 reshape_reshape.6
  24.1 4.1 constant_dynamic-slice_fusion.5
  30.4 2.5 collective-permute-start.1
  35.1 12.3 %collective-permute-done.1 = bf16[2,256,3,192]{1,3,2,0:T(8,128)(2,1)} collective-permute-done((bf16[2,256,3,192]{1,3,2,0:T(8,128)(2,1)}, bf16[2,256,3,192]{1,3,2,0:T(8,128)(2,1)}, u32[]{:S(2)}, u32[]{:S(2)}) %collective-permute-start.1) | collective-permute-done | bytes 589856 | tf_op jit(solution)/shard_map/ppermute | solution.py:29
  47.4 12.3 %collective-permute-done.2 = bf16[2,256,3,192]{1,3,2,0:T(8,128)(2,1)} collective-permute-done((bf16[2,256,3,192]{1,3,2,0:T(8,128)(2,1)}, bf16[2,256,3,192]{1,3,2,0:T(8,128)(2,1)}, u32[]{:S(2)}, u32[]{:S(2)}) %collective-permute-start.2) | collective-permute-done | bytes 589856 | tf_op jit(solution)/shard_map/ppermute | solution.py:29
  59.7 3.1 pad_maximum_fusion
  62.8 3.8 gather_fusion
  66.6 4.9 copy.117
  71.5 5.5 reshape_reshape.7
  76.9 3.1 slice_bitcast_fusion
  80.0 49.0 %while.22 = (s32[]{:T(128)}, bf16[2,1024,3,64]{1,3,2,0:T(8,128)(2,1)}, f32[2,3,1024]{2,1,0:T(4,128)}, bf16[2,1024,3,64]{1,3,2,0:T(8,128)(2,1)}, s32[2,1024]{1,0:...) while((s32[]{:T(128)}, ...), condition=%wide.region_3.4_spmd, body=%wide.region_0.3_spmd.sunk | while | flops 844297216 | bytes 46787188 | solution.py:121
  80.9 8.2 fusion.118
  89.1 7.4 fusion.119
  97.1 7.5 fusion.120
  105.3 8.2 fusion.118
  113.5 7.4 fusion.119
  121.5 7.5 fusion.120
  129.0 3.6 copy.118
  132.7 4.4 all-to-all-start
  144.2 7.4 all-to-all-done
  151.6 3.8 copy.133
  155.4 1.9 copy.120
  158.5 2.6 fusion.79
  161.5 19.7 %multiply_convert_fusion.1 = (bf16[512,3072]{1,0:T(8,128)(2,1)S(1)}, f32[512,3072]{1,0:T(8,128)}, f32[512,3072]{1,0:T(8,128)}) fusion(f32[3072]{0:T(1024)S(1)} %copy-done.26, bf16[768,3072]{1,0:T(8,128)(2,1)} %param.29, f32[512,768]{1,0:T(8,128)S(1)} %get-tuple-element.253, f32[768]{0:T(1024)S(1)} %copy-done.30, f32[768]{0:T(1024)S(1)} %copy-done.24, ...), kind=kOutput, calls=%fused_computation.69 | convolution fusion | flops 2521694208 | bytes 22042624 | tf_op jit(solution)/shard_map/dot_general | solution.py:133
  181.2 2.8 fusion.80
  187.3 9.8 %convert_reduce_fusion = (f32[3072]{0:T(1024)}, bf16[512,3072]{1,0:T(8,128)(2,1)}) fusion(f32[512,3072]{1,0:T(8,128)} %get-tuple-element.239, bf16[3072,768]{1,0:T(8,128)(2,1)S(1)} %bitcast.211, f32[512,768]{1,0:T(8,128)S(1)} %get-tuple-element.237, f32[512]{0:T(512)S(1)} %negate_multiply_fusion.2, f32[512,3072]{1,0:T(8,128)} %get-tuple-element.254, ...), kind=kOutput, calls=%fused_computation.67 | convolution fusion | flops 2443441152 | bytes 22046720 | tf_op jit(solution)/shard_map/to,io->ti/dot_general | solution.py:150
  197.1 5.7 multiply_reduce_fusion.1
  206.4 3.0 copy.121
  209.4 4.2 all-to-all-start.1
  213.7 4.0 fusion.71
  217.7 7.6 all-to-all-done.1
  228.0 2.7 reshape.295
  230.7 57.5 %while.23 = (s32[]{:T(128)}, bf16[2,1024,3,3,64]{1,4,3,2,0:T(8,128)(2,1)}, bf16[2,1024,3,64]{1,3,2,0:T(8,128)(2,1)}, s32[2,1024]{1,0:T(2,128)S(1)}, bf16[2,1024,...) while((s32[]{:T(128)}, ...), condition=%wide.region_14.15_spmd, body=%wide.region_12.14_spmd.sunk | while | flops 2066019328 | bytes 119119104 | solution.py:169
  230.7 3.1 fusion.129
  235.2 7.2 multiply_reduce_fusion.6
  242.4 7.1 multiply_convert_fusion.3
  250.8 2.8 fusion.131
  253.6 4.8 fusion.130
  259.5 3.1 fusion.129
  264.0 7.2 multiply_reduce_fusion.6
  271.2 7.0 multiply_convert_fusion.3
  279.5 2.8 fusion.131
  282.3 4.8 fusion.130
  288.2 8.6 copy.124
  296.9 42.5 %all_to_all.45 = bf16[2,1024,3,192]{3,0,2,1:T(2,128)(2,1)} all-to-all(bf16[2,1024,3,192]{3,0,2,1:T(2,128)(2,1)} %copy.124), channel_id=1, replica_groups=mesh['batch'=8,'seq'=4] {'seq'}, dimensions={1} | all-to-all | bytes 4718592 | tf_op jit(solution)/shard_map/all_to_all | solution.py:170
  339.3 9.0 %copy.134 = bf16[2,4,256,3,192]{2,1,4,3,0:T(4,128)(2,1)} copy(bf16[2,4,256,3,192]{4,0,3,2,1:T(2,128)(2,1)} %bitcast.194) | data formatting | bytes 4718592 | tf_op jit(solution)/shard_map/all_to_all | solution.py:170
  348.4 4.1 copy.126
  354.3 5.0 convolution_bitcast_fusion
  360.0 9.7 %fusion.69 = f32[3072,768]{0,1:T(8,128)} fusion(bf16[512,3072]{1,0:T(8,128)(2,1)} %copy-done.14, f32[512,768]{1,0:T(8,128)} %copy-done.7, f32[512]{0:T(512)S(1)} %copy-done.22), kind=kOutput, calls=%fused_computation.139 | convolution fusion | flops 2416705536 | bytes 14157824 | tf_op jit(solution)/shard_map/ti,to->io/dot_general | solution.py:149
  370.5 9.4 %fusion.72 = f32[768,3072]{1,0:T(8,128)} fusion(bf16[512,3072]{1,0:T(8,128)(2,1)} %get-tuple-element.259, f32[512,768]{1,0:T(8,128)} %copy-done.12, f32[768]{0:T(1024)} %convert_element_type.101, f32[768]{0:T(1024)S(1)} %copy-done.25, f32[512]{0:T(512)S(1)} %copy-done.28, f32[512]{0:T(512)S(1)} %copy-done.20), kind=kOutput, calls=%fused_computation.142 | convolution fusion | flops 2417885184 | bytes 14166016 | tf_op jit(solution)/shard_map/ti,to->io/dot_general | solution.py:154
  380.0 2.2 copy.137
  382.3 41.1 %reduce-scatter.13.cloned.1.call-done = f32[768,576]{0,1:T(8,128)} async-done(((f32[768,2304]{0,1:T(8,128)}), f32[768,576]{0,1:T(8,128)}) %reduce-scatter.13.cloned.1.call-update) | async-done | bytes 1769488 | tf_op jit(solution)/shard_map/reduce_scatter | solution.py:185
  423.4 2.9 copy.135
  426.3 78.1 %reduce-scatter.21.cloned.1.call-done = f32[3072,192]{0,1:T(8,128)} async-done(((f32[3072,768]{0,1:T(8,128)}), f32[3072,192]{0,1:T(8,128)}) %reduce-scatter.21.cloned.1.call-update) | async-done | bytes 2359312 | tf_op jit(solution)/shard_map/reduce_scatter | solution.py:188
  504.6 80.8 %reduce-scatter.17.cloned.1.call-done = f32[768,768]{1,0:T(8,128)} async-done(((f32[768,3072]{1,0:T(8,128)}), f32[768,768]{1,0:T(8,128)}) %reduce-scatter.17.cloned.1.call-update) | async-done | bytes 2359312 | tf_op jit(solution)/shard_map/reduce_scatter | solution.py:187
  586.8 2.2 add_reduce_fusion.1
  591.5 41.3 %all-reduce = (f32[768]{0:T(1024)}, f32[768]{0:T(1024)}, f32[768]{0:T(1024)}, f32[768]{0:T(1024)}, f32[768]{0:T(1024)}, /*index=5*/f32[3072]{0:T(1024)}, f32[768]{0:T(1024)}, f32[768]{0:T(1024)}, f32[768]{0:T(1024)}) all-reduce(f32[768]{0:T(1024)} %get-tuple-element.193, ...), channel_id=1, replica_groups=mesh['batch'=8,'seq'=4] {'batch','seq'}, use_global_device_ids=true, to_apply=%region_18.19 | all-reduce | flops 9216 | bytes 73728 | tf_op jit(solution)/shard_map/psum | solution.py:197
  632.8 5.3 convolution_add_fusion.1
  638.1 13.7 %reduce-scatter.27.cloned.1.call-done = f32[96,192]{1,0:T(8,128)} async-done(((f32[768,192]{1,0:T(8,128)}), f32[96,192]{1,0:T(8,128)}) %reduce-scatter.27.cloned.1.call-update) | async-done | bytes 73744
  651.8 69.9 %reduce-scatter.25.cloned.1.call-done = f32[96,576]{1,0:T(8,128)} async-done(((f32[768,576]{1,0:T(8,128)}), f32[96,576]{1,0:T(8,128)}) %reduce-scatter.25.cloned.1.call-update) | async-done | bytes 221200
  721.7 72.0 %reduce-scatter.23.cloned.1.call-done = f32[384,192]{0,1:T(8,128)} async-done(((f32[3072,192]{0,1:T(8,128)}), f32[384,192]{0,1:T(8,128)}) %reduce-scatter.23.cloned.1.call-update) | async-done | bytes 294928 | tf_op jit(solution)/shard_map/reduce_scatter | solution.py:194
  793.7 72.3 %reduce-scatter.19.cloned.1.call-done = f32[96,768]{1,0:T(8,128)} async-done(((f32[768,768]{1,0:T(8,128)}), f32[96,768]{1,0:T(8,128)}) %reduce-scatter.19.cloned.1.call-update) | async-done | bytes 294928 | tf_op jit(solution)/shard_map/reduce_scatter | solution.py:193
  (165 shorter events, 42.2 us)
Async XLA Ops:
  7.2 2.0 copy-start
  29.1 6.1 collective-permute-start
  30.4 17.0 %collective-permute-start.1 = (bf16[2,256,3,192]{1,3,2,0:T(8,128)(2,1)}, bf16[2,256,3,192]{1,3,2,0:T(8,128)(2,1)}, u32[]{:S(2)}, u32[]{:S(2)}) collective-permute-start(bf16[2,256,3,192]{1,3,2,0:T(8,128)(2,1)} %bitcast.147), channel_id=1, source_target_pairs={{0,2},{1,3},{2,0},{3,1},{4,6},{5,7},{6,4},{7,5},{8,10},{9,11},{10,... | collective-permute-start | bytes 1769480 | tf_op jit(solution)/shard_map/ppermute | solution.py:29
  33.8 25.8 %collective-permute-start.2 = (bf16[2,256,3,192]{1,3,2,0:T(8,128)(2,1)}, bf16[2,256,3,192]{1,3,2,0:T(8,128)(2,1)}, u32[]{:S(2)}, u32[]{:S(2)}) collective-permute-start(bf16[2,256,3,192]{1,3,2,0:T(8,128)(2,1)} %bitcast.146), channel_id=1, source_target_pairs={{0,3},{1,2},{2,1},{3,0},{4,7},{5,6},{6,5},{7,4},{8,11},{9,10},{10,... | collective-permute-start | bytes 1769480 | tf_op jit(solution)/shard_map/ppermute | solution.py:29
  76.9 3.1 copy-start.16
  89.1 8.0 copy-start.8
  113.5 8.0 copy-start.8
  129.0 11.9 %copy-start.29 = (bf16[3072]{0:T(1024)(128)(2,1)S(1)}, bf16[3072]{0:T(1024)(128)(2,1)}, u32[]{:S(2)}) copy-start(bf16[3072]{0:T(1024)(128)(2,1)} %param.30) | copy-start | bytes 18436
  132.7 19.0 %all-to-all-start = ((bf16[2,1024,192]{2,0,1:T(2,128)(2,1)}), bf16[2,1024,192]{2,0,1:T(2,128)(2,1)}, u32[]{:S(2)}, u32[]{:S(2)}) async-start(bf16[2,1024,192]{2,0,1:T(2,128)(2,1)} %copy.118), calls=%async_computation | async-start | bytes 2097152 | tf_op jit(solution)/shard_map/all_to_all | solution.py:123
  157.5 0.9 copy-start.13
  157.5 3.9 copy-start.24
  157.5 3.9 copy-start.26
  157.6 3.9 copy-start.30
  158.5 22.7 %slice-start = ((s8[4718592]{0:T(1024)(128)(4,1)}), s8[4194304]{0:T(1024)(128)(4,1)S(1)}, s32[]{:S(2)}) async-start(s8[4718592]{0:T(1024)(128)(4,1)} %bitcast.210), calls=%async_computation.19 | async-start | bytes 8388608
  161.0 41.7 %copy-start.12 = (f32[512,768]{1,0:T(8,128)}, f32[512,768]{1,0:T(8,128)S(1)}, u32[]{:S(2)}) copy-start(f32[512,768]{1,0:T(8,128)S(1)} %get-tuple-element.253) | copy-start | bytes 4718596
  161.1 41.7 %copy-start.19 = (f32[512]{0:T(512)}, f32[512]{0:T(512)S(1)}, u32[]{:S(2)}) copy-start(f32[512]{0:T(512)S(1)} %broadcast_multiply_fusion.1) | copy-start | bytes 6148
  161.4 41.4 %copy-start.27 = (f32[512]{0:T(512)}, f32[512]{0:T(512)S(1)}, u32[]{:S(2)}) copy-start(f32[512]{0:T(512)S(1)} %fusion.66) | copy-start | bytes 6148
  161.4 19.7 %copy-start.31 = (f32[768]{0:T(1024)S(1)}, f32[768]{0:T(1024)}, u32[]{:S(2)}) copy-start(f32[768]{0:T(1024)} %convert_element_type.105) | copy-start | bytes 9220
  161.4 19.7 %slice-start.1 = ((s8[4718592]{0:T(1024)(128)(4,1)}), s8[524288]{0:T(1024)(128)(4,1)S(1)}, s32[]{:S(2)}) async-start(s8[4718592]{0:T(1024)(128)(4,1)} %bitcast.210), calls=%async_computation.20 | async-start | bytes 1048576
  181.1 2.9 copy-start.14
  181.2 3.2 copy-start.11
  185.6 11.4 %slice-start.2 = ((s8[4718592]{0:T(1024)(128)(4,1)}), s8[4194304]{0:T(1024)(128)(4,1)S(1)}, s32[]{:S(2)}) async-start(s8[4718592]{0:T(1024)(128)(4,1)} %bitcast.212), calls=%async_computation.21 | async-start | bytes 8388608
  187.3 9.8 %copy-start.7 = (f32[512,768]{1,0:T(8,128)}, f32[512,768]{1,0:T(8,128)S(1)}, u32[]{:S(2)}) copy-start(f32[512,768]{1,0:T(8,128)S(1)} %get-tuple-element.237) | copy-start | bytes 4718596
  187.3 9.8 %copy-start.21 = (f32[512]{0:T(512)}, f32[512]{0:T(512)S(1)}, u32[]{:S(2)}) copy-start(f32[512]{0:T(512)S(1)} %negate_multiply_fusion.2) | copy-start | bytes 6148
  187.3 9.8 %slice-start.3 = ((s8[4718592]{0:T(1024)(128)(4,1)}), s8[524288]{0:T(1024)(128)(4,1)S(1)}, s32[]{:S(2)}) async-start(s8[4718592]{0:T(1024)(128)(4,1)} %bitcast.212), calls=%async_computation.22 | async-start | bytes 1048576
  202.8 1.8 copy-start.32
  203.4 1.1 copy-start.6
  203.5 10.2 %copy-start.17 = (f32[512]{0:T(512)}, f32[512]{0:T(512)S(1)}, u32[]{:S(2)}) copy-start(f32[512]{0:T(512)S(1)} %negate_multiply_fusion.1) | copy-start | bytes 6148
  209.4 15.9 %all-to-all-start.1 = ((bf16[2,256,768]{1,0,2:T(2,128)(2,1)}), bf16[2,256,768]{1,0,2:T(2,128)(2,1)}, u32[]{:S(2)}, u32[]{:S(2)}) async-start(bf16[2,256,768]{1,0,2:T(2,128)(2,1)} %copy.121), calls=%async_computation.1 | async-start | bytes 1572864 | tf_op jit(solution)/shard_map/all_to_all | solution.py:165
  213.6 166.4 %reduce-scatter.15.cloned.1.call-start = ((), (), s32[]{:S(2)}) async-start(), calls=%async_computation.12 | async-start | bytes 2949120 | tf_op jit(solution)/shard_map/reduce_scatter | solution.py:186
  217.7 205.7 %reduce-scatter.13.cloned.1.call-start = ((), (), s32[]{:S(2)}) async-start(), calls=%async_computation.11 | async-start | bytes 8847360 | tf_op jit(solution)/shard_map/reduce_scatter | solution.py:185
  230.7 4.5 copy-start.9
  230.7 4.5 copy-start.10
  242.4 7.1 copy-start.2
  249.5 1.2 copy-start.3
  253.6 4.8 copy-start.1
  259.5 4.5 copy-start.9
  259.5 4.5 copy-start.10
  271.2 7.0 copy-start.2
  278.2 1.2 copy-start.3
  282.2 4.8 copy-start.1
  352.5 1.9 copy-start.15
  353.0 1.4 copy-start.4
  359.3 0.7 copy-start.22
  359.3 145.1 %reduce-scatter.21.cloned.1.call-start = ((), (), s32[]{:S(2)}) async-start(), calls=%async_computation.15 | async-start | bytes 11796480 | tf_op jit(solution)/shard_map/reduce_scatter | solution.py:188
  369.7 0.7 copy-start.20
  369.7 0.7 copy-start.25
  369.7 0.8 copy-start.28
  369.7 215.7 %reduce-scatter.17.cloned.1.call-start = ((), (), s32[]{:S(2)}) async-start(), calls=%async_computation.13 | async-start | bytes 11796480 | tf_op jit(solution)/shard_map/reduce_scatter | solution.py:187
  379.9 271.9 %reduce-scatter.27.cloned.1.call-start = ((), (), s32[]{:S(2)}) async-start(), calls=%async_computation.18 | async-start | bytes 884736
  382.2 339.5 %reduce-scatter.25.cloned.1.call-start = ((), (), s32[]{:S(2)}) async-start(), calls=%async_computation.17 | async-start | bytes 2211840
  426.3 367.4 %reduce-scatter.23.cloned.1.call-start = ((), (), s32[]{:S(2)}) async-start(), calls=%async_computation.16 | async-start | bytes 2654208 | tf_op jit(solution)/shard_map/reduce_scatter | solution.py:194
  504.5 84.5 %copy-start.18 = (f32[512]{0:T(512)S(1)}, f32[512]{0:T(512)}, u32[]{:S(2)}) copy-start(f32[512]{0:T(512)} %copy-done.17) | copy-start | bytes 6148
  504.5 361.5 %reduce-scatter.19.cloned.1.call-start = ((), (), s32[]{:S(2)}) async-start(), calls=%async_computation.14 | async-start | bytes 2654208 | tf_op jit(solution)/shard_map/reduce_scatter | solution.py:193
  585.4 6.1 copy-start.23
  585.4 5.2 copy-start.5
Sparse Core Ops, SparseCore 0:
  217.8 34.7 reduce-scatter.14
  359.5 63.8 reduce-scatter.12
  426.0 78.4 reduce-scatter.20
  506.9 78.3 reduce-scatter.16
  589.1 62.6 reduce-scatter.26
  656.1 65.5 reduce-scatter.24
  725.8 67.8 reduce-scatter.22
  797.7 68.2 reduce-scatter.18
